TPU v7x, 512 devices: a whole 4x8x8 slice. The times are simulated.
512 devices in a mesh: row: 8 (over z_lo, x), col: 16 (over y, core), freq: 4 (over z_hi).
Axes of the slice: x: 4, y: 8, z: 8 (z_hi: 4, z_lo: 2; z = z_hi * 2 + z_lo), core: 2. Of those that a mesh axis runs over, the one named last changes fastest.
Arguments:
- covariance: bfloat16 [16, 2, 4096, 4096], P('freq', None, 'row', 'col'), may hold values from -30 to 30, as said below
- replica_table: bfloat16 [16, 2, 4096, 512], P('freq', None, 'col'), may hold values from -18 to 18
- slab_index: int32 [384], replicated, may hold values from 0 to 511
Outputs:
- power: float32 [16, 384], P('freq', ('row', 'col'))
- surface: float32 [384], P(('row', 'col'))
Inputs may be any that keep to these rules, and one draw needn't show every extreme that they name: For each frequency, covariance is Hermitian: its real part is symmetric and its imaginary part antisymmetric, and the whole is positive definite.
All inputs are finite; a program needn't handle non-finite values.
Results may differ from a plain program's by a relative error of at most 0.0003.
Values may be sent and summed in bfloat16 or wider, within the bound.
A program may use at most 64 MiB of HBM per device.

v0:
```python
import jax
import jax.numpy as jnp
from jax import lax
from jax.sharding import PartitionSpec as P

FREQ = 16


def broadcast(shard, axis, root):
    mine = lax.axis_index(axis) == root
    return lax.psum(jnp.where(mine, shard, jnp.zeros_like(shard)), axis)


def local(covariance, replica_table, slab_index):
    local_slab = jnp.take(replica_table, slab_index, axis=3)
    row_index = lax.axis_index("row")
    first_half = broadcast(local_slab, "col", 2 * row_index)
    second_half = broadcast(local_slab, "col", 2 * row_index + 1)
    row_slab = jnp.concatenate([first_half, second_half], axis=2)
    freqs = covariance.shape[0]
    rows_block = covariance.shape[2]
    cols_block = covariance.shape[3]
    slab = slab_index.shape[0]
    stacked = covariance.reshape(freqs, 2 * rows_block, cols_block)
    right_side = jnp.concatenate([local_slab[:, 0], local_slab[:, 1]], axis=2)
    image = jnp.einsum("fij,fjs->fis", stacked, right_side, preferred_element_type=jnp.float32)
    real_a = image[:, :rows_block, :slab]
    real_b = image[:, :rows_block, slab:]
    imag_a = image[:, rows_block:, :slab]
    imag_b = image[:, rows_block:, slab:]
    image_real = real_a - imag_b
    image_imag = real_b + imag_a
    quad = jnp.sum(
        row_slab[:, 0].astype(jnp.float32) * image_real
        + row_slab[:, 1].astype(jnp.float32) * image_imag,
        axis=1,
    )
    share = cols_block // lax.axis_size("row")
    own_piece = lax.dynamic_slice_in_dim(local_slab, row_index * share, share, 2).astype(
        jnp.float32
    )
    weight = jnp.sum(own_piece * own_piece, axis=(1, 2))
    quad_total, weight_total = (
        lax.psum_scatter(quad, ("row", "col"), scatter_dimension=1, tiled=True),
        lax.psum_scatter(weight, ("row", "col"), scatter_dimension=1, tiled=True),
    )
    power = quad_total / weight_total
    surface = lax.psum(jnp.sum(power, axis=0), "freq") / FREQ
    return (power, surface)


def solution(mesh):
    in_specs = (P("freq", None, "row", "col"), P("freq", None, "col", None), P())
    out_specs = (P("freq", ("row", "col")), P(("row", "col")))
    return jax.shard_map(local, mesh=mesh, in_specs=in_specs, out_specs=out_specs, check_vma=False)
```

profile of v0, /device:TPU:1, one launch (start us, length us, event | category | flops | bytes accessed | tf_op | source)
XLA Modules:
  0.0 726.7 jit_solution(14267626325725935616)
XLA Ops:
  7.2 0.0 copy-start
  7.2 0.0 all-reduce.6.cloned.1.call-start
  7.2 0.8 compare_and_fusion
  8.1 0.7 compare_select_fusion
  8.7 4.3 copy.7
  13.0 4.8 gather_fusion
  17.9 3.0 broadcast_select_fusion
  20.9 1.2 copy-done.1
  22.1 1.3 broadcast_select_fusion.1
  23.4 0.0 all-reduce.6.cloned.1.call-update
  23.4 1.3 dynamic-slice.1
  25.3 1.6 multiply_reduce_fusion
  27.0 1.5 slice_bitcast_fusion.3
  28.4 0.0 copy-done
  28.5 6.4 convolution_bitcast_fusion
  34.9 117.4 %all-reduce.6.cloned.1.call-done = (bf16[4,2,256,384]{2,3,0,1:T(8,128)(2,1)}, bf16[4,2,256,384]{2,3,0,1:T(8,128)(2,1)}) async-done(((bf16[4,2,256,384]{2,3,0,1:T(8,128)(2,1)}, bf16[4,2,256,384]{2,3,0,1:T(8,128)(2,1)}), (bf16[4,2,256,384]{2,3,0,1:T(8,128)(2,1)}, bf16[4,2,256,384]{2,3,0,1:T(8,128)(2,1)})) %all-reduce.6.cloned.1.call-update) | async-done | bytes 3145744 | tf_op jit(solution)/shard_map/psum | solution.py:11
  152.3 1.7 constant_dynamic-update-slice_fusion.1
  153.9 0.2 copy-done.2
  154.2 0.1 constant_dynamic-update-slice_fusion
  154.3 5.2 fusion.2
  159.5 548.8 %all-reduce.2 = (f32[4,384]{1,0:T(4,128)S(1)}, f32[4,384]{1,0:T(4,128)S(1)}) all-reduce(f32[4,384]{1,0:T(4,128)S(1)} %bitcast.29, f32[4,384]{1,0:T(4,128)S(1)} %fusion.2), channel_id=3, replica_groups=mesh['row'=8,'col'=16,'freq'=4] {'row','col'}, use_global_device_ids=true, to_apply=%region_5.6.clone | all-reduce | flops 3072 | bytes 24576
  708.3 0.7 fusion.8
  709.0 10.3 %psum.23 = f32[3]{0:T(128)S(1)} all-reduce(f32[3]{0:T(128)S(1)} %get-tuple-element.6), channel_id=1, replica_groups=mesh['row'=8,'col'=16,'freq'=4] {'freq'}, use_global_device_ids=true, to_apply=%region_7.8 | all-reduce | flops 3 | bytes 24 | tf_op jit(solution)/shard_map/psum | solution.py:48
  719.3 0.5 broadcast_multiply_fusion
  (3 shorter events, 0.0 us)
Async XLA Ops:
  7.2 21.3 %copy-start = (bf16[4,2,512,256]{3,2,1,0:T(8,128)(2,1)S(1)}, bf16[4,2,512,256]{3,2,1,0:T(8,128)(2,1)}, u32[]{:S(2)}) copy-start(bf16[4,2,512,256]{3,2,1,0:T(8,128)(2,1)} %param.3) | copy-start | bytes 6291460
  7.2 145.1 %all-reduce.6.cloned.1.call-start = ((), (), s32[]{:S(2)}) async-start(), calls=%async_computation | async-start | bytes 6291456 | tf_op jit(solution)/shard_map/psum | solution.py:11
  20.9 1.2 copy-start.1
  152.3 1.9 copy-start.2
Sparse Core Ops, SparseCore 0:
  23.5 128.7 all-reduce.5
where the time goes:
time: 733 us; the launch traced here: 727 us
  blocking collectives  559 us (76%)
  waiting for transfers between devices  117 us (16%)
  local copies, waits for them, and re-layouts  15 us (2%)
  between operations  14.7 us (2%)
  other arithmetic  13.9 us (2%)
    unnamed x1, blocking collectives  549 us
    psum x1, waiting for transfers between devices, broadcast(): return lax.psum(jnp.where(mine, shard, jnp.zeros_like(shard)), axis)  117 us
  transfers between devices with their start and end apart: 1, of which 1 were waited for; matrix products, arithmetic and copies ran while one was open for 1% of the time, Pallas kernels for 0%

commit v1 on v0

v1 whole, which is shorter than its diff:
```python
import functools

import jax
import jax.numpy as jnp
from jax import lax
from jax.experimental import pallas as pl
from jax.experimental.pallas import tpu as pltpu
from jax.sharding import PartitionSpec as P

MESH = pl.DeviceIdType.MESH
F32 = jnp.float32
BF16 = jnp.bfloat16
NCH = 16


def kernel(sizes, cov, tbl, idx, pow_ref, surf_ref,
           T, C, X, OH, IM, B, S, ACC, WT, R1, R2, R3,
           tsem, csem, b_recv, s_recv, up_send, dn_send, z_send, s_send,
           r1_send, r1_recv, r2_send, r2_recv, r3_send, r3_recv):
    n_row, n_col, n_freq, ch, slab, table, total_freqs = sizes
    cr = ch // NCH
    r = lax.axis_index("row")
    c = lax.axis_index("col")
    q = lax.axis_index("freq")
    y = c // 2
    k = c % 2
    zl = r // 4
    d = (y - r + 8) % 8
    up = (r, (c + 2) % 16, q)
    down = (r, (c + 14) % 16, q)
    mate = ((r + 4) % 8, c, q)
    sib = (r, c + 1 - 2 * k, q)

    barrier = pltpu.get_barrier_semaphore()
    for j in range(1, n_col):
        pl.semaphore_signal(barrier, inc=1, device_id=(r, (c + j) % n_col, q), device_id_type=MESH)
    for j in range(1, n_row):
        pl.semaphore_signal(barrier, inc=1, device_id=((r + j) % n_row, c, q), device_id_type=MESH)
    for j in range(1, n_freq):
        pl.semaphore_signal(barrier, inc=1, device_id=(r, c, (q + j) % n_freq), device_id_type=MESH)

    ends = (d == 0) | (d == 4)
    base = jnp.where(d >= 5, 2, 0)
    n_slots = jnp.where(d == 0, 4, 2)

    def freq_of(i):
        first = jnp.where(i == 0, base + zl, jnp.where(ends, 2 + zl, base + 1 - zl))
        return jnp.where(i < 2, first, jnp.where(i == 2, 1 - zl, 3 - zl))

    def table_copy(i):
        return pltpu.make_async_copy(tbl.at[freq_of(i)], T.at[i], tsem.at[i])

    def cov_copies(i):
        out = []
        for part in range(2):
            for half in range(2):
                rows = pl.ds(pl.multiple_of((k if half == 0 else 1 - k) * ch, ch), ch)
                out.append(pltpu.make_async_copy(
                    cov.at[freq_of(i), part, rows, :],
                    C.at[i, pl.ds(half * ch, ch), pl.ds(part * ch, ch)],
                    csem.at[i, 2 * part + half]))
        return out

    def start_table(i, carry):
        table_copy(i).start()
        return carry

    def start_cov(i, carry):
        for copy in cov_copies(i):
            copy.start()
        return carry

    lax.fori_loop(0, n_slots, start_table, 0)
    lax.fori_loop(0, n_slots, start_cov, 0)

    points = lax.broadcasted_iota(jnp.int32, (table, slab), 0)
    OH[...] = jnp.where(points == idx[...], 1.0, 0.0).astype(BF16)
    ACC[...] = jnp.zeros_like(ACC)
    WT[...] = jnp.zeros_like(WT)

    def chunk(j):
        return pl.ds(pl.multiple_of(j * cr, cr), cr)

    def remote(src, dst, send, recv, to):
        return pltpu.make_async_remote_copy(
            src_ref=src, dst_ref=dst, send_sem=send, recv_sem=recv, device_id=to, device_id_type=MESH)

    to_up = jnp.where(d <= 3, 0, 2)
    to_down = jnp.where((d == 0) | (d >= 6), 0, jnp.where(d == 5, 1, 2))
    from_down = jnp.where(d <= 4, 0, 2)
    from_up = jnp.where(d >= 5, 0, jnp.where(d == 4, 1, 2))

    def send_up(src, j):
        return remote(src, B.at[to_up, chunk(j)], up_send, b_recv.at[to_up, j], up)

    def send_down(src, j):
        return remote(src, B.at[to_down, chunk(j)], dn_send, b_recv.at[to_down, j], down)

    def send_mate(src, j):
        return remote(src, B.at[1, chunk(j)], z_send, b_recv.at[1, j], mate)

    def send_sib(src, i, j):
        return remote(src, S.at[i, chunk(j)], s_send.at[i], s_recv.at[i, j], sib)

    def own_rows(i, j):
        return X.at[i, chunk(j), :]

    def gather(i, carry):
        table_copy(i).wait()
        both = jnp.dot(T[i].reshape(2 * ch, table), OH[...], preferred_element_type=F32)
        a, b = both[:ch], both[ch:]
        na, nb = a.astype(BF16), b.astype(BF16)
        X[i, 0:ch, 0:slab] = na
        X[i, 0:ch, slab:2 * slab] = nb
        X[i, ch:2 * ch, 0:slab] = -nb
        X[i, ch:2 * ch, slab:2 * slab] = na

        @pl.when(d == 0)
        def _():
            WT[i] = jnp.sum((a * a + b * b).reshape(ch // 8, 8, slab), axis=0)

        @pl.when(i == 0)
        def _():
            pl.semaphore_wait(barrier, n_col + n_row + n_freq - 3)

        @pl.when(ends & (i == 0))
        def _():
            def go(j, carry):
                send_up(own_rows(i, j), j).start()
                return carry
            lax.fori_loop(0, NCH, go, 0)

        @pl.when(ends & (i == 1))
        def _():
            def go(j, carry):
                send_down(own_rows(i, j), j).start()
                return carry
            lax.fori_loop(0, NCH, go, 0)

        @pl.when(d == 0)
        def _():
            def go(j, carry):
                send_sib(own_rows(i, j), i, j).start()
                return carry
            lax.fori_loop(0, NCH, go, 0)

        return carry

    lax.fori_loop(0, n_slots, gather, 0)

    def image(i, carry):
        for copy in cov_copies(i):
            copy.wait()
        IM[i] = jnp.dot(C[i], X[i], preferred_element_type=F32)
        return carry

    lax.fori_loop(0, n_slots, image, 0)

    def wait_in(slot, j):
        remote(B.at[slot, chunk(j)], B.at[slot, chunk(j)], z_send, b_recv.at[slot, j], sib).wait_recv()

    def wait_sib(i, j):
        remote(S.at[i, chunk(j)], S.at[i, chunk(j)], z_send, s_recv.at[i, j], sib).wait_recv()

    def fold(w, im):
        return jnp.sum((w.astype(F32) * im).reshape(cr // 8, 8, 2 * slab), axis=0)

    def combine(own, i, j):
        mine = fold(own[...], IM[i, chunk(j), :])
        other = pl.ds(pl.multiple_of(ch + j * cr, cr), cr)
        ACC[i] += mine + fold(S[i, chunk(j), :], IM[i, other, :])

    @pl.when(d == 0)
    def _():
        def each(m, carry):
            i, j = m // NCH, m % NCH
            wait_sib(i, j)
            combine(own_rows(i, j), i, j)
            return carry
        lax.fori_loop(0, 4 * NCH, each, 0)

    hops = jnp.where(d <= 4, d, 8 - d)

    @pl.when(d != 0)
    def _():
        lag_p = jnp.where(d <= 4, d, d - 4) - 1
        lag_m = jnp.where(d >= 4, 8 - d, 4 - d) - 1
        lag_1 = jnp.where(d == 4, 4, hops + 1)

        def within(j):
            return (j >= 0) & (j < NCH)

        def step(t, carry):
            jp = t - lag_p

            @pl.when(within(jp))
            def _():
                wait_in(from_down, jp)
                here = B.at[from_down, chunk(jp)]

                @pl.when((d != 4) & (d != 7))
                def _():
                    send_up(here, jp).start()

                @pl.when(d <= 4)
                def _():
                    send_sib(here, 0, jp).start()

                @pl.when(d >= 5)
                def _():
                    send_mate(here, jp).start()

            jm = t - lag_m

            @pl.when(within(jm))
            def _():
                wait_in(from_up, jm)
                here = B.at[from_up, chunk(jm)]

                @pl.when((d != 4) & (d != 1))
                def _():
                    send_down(here, jm).start()

                @pl.when(d >= 4)
                def _():
                    send_sib(here, from_up, jm).start()

                @pl.when(d <= 3)
                def _():
                    send_mate(here, jm).start()

            jz = t - hops

            @pl.when(within(jz) & (d != 4))
            def _():
                wait_in(1, jz)
                send_sib(B.at[1, chunk(jz)], 1, jz).start()

            j0 = t - hops

            @pl.when(within(j0))
            def _():
                wait_sib(0, j0)
                combine(B.at[0, chunk(j0)], 0, j0)

            j1 = t - lag_1

            @pl.when(within(j1))
            def _():
                wait_sib(1, j1)
                combine(B.at[1, chunk(j1)], 1, j1)

            return carry

        lax.fori_loop(0, NCH + 4, step, 0)

    scale = jnp.where(d == 0, 1.0, 2.0).astype(F32)
    rows8 = lax.broadcasted_iota(jnp.int32, (8, slab), 0)
    part = jnp.zeros((8, slab), F32)
    for i in range(4):
        live = i < n_slots
        sums = (ACC[i, :, 0:slab] + ACC[i, :, slab:2 * slab]) * scale
        quad = jnp.sum(sums, axis=0, keepdims=True)
        norm = jnp.sum(WT[i], axis=0, keepdims=True)
        f = freq_of(i)
        part = jnp.where((rows8 == f) & live, quad, part)
        part = jnp.where((rows8 == f + 4) & live, norm, part)
    R1[0] = part

    ones = []
    for j in range(1, n_row):
        copy = remote(R1.at[0], R1.at[j], r1_send.at[j], r1_recv.at[j], ((r + j) % n_row, c, q))
        copy.start()
        ones.append(copy)

    def sent(ref, sem):
        remote(ref, ref, sem, b_recv.at[0, 0], sib).wait_send()

    whole = S.at[0]

    @pl.when((d != 4) & (d != 7) | ends)
    def _():
        sent(whole, up_send)

    @pl.when((d != 4) & (d != 1) | ends)
    def _():
        sent(whole, dn_send)

    @pl.when(~ends)
    def _():
        sent(whole, z_send)

    def sib_sent(i, carry):
        sent(whole, s_send.at[i])
        return carry

    lax.fori_loop(0, n_slots, sib_sent, 0)

    for copy in ones:
        copy.wait_recv()
    summed = R1[0]
    for j in range(1, n_row):
        summed += R1[j]
    share = slab // n_row
    mine = pltpu.roll(summed, (slab - share * r) % slab, 1)
    R2[0] = mine[:, 0:128]
    twos = []
    for j in range(1, n_col):
        copy = remote(R2.at[0], R2.at[j], r2_send.at[j], r2_recv.at[j], (r, (c + j) % n_col, q))
        copy.start()
        twos.append(copy)
    for copy in ones:
        copy.wait_send()
    for copy in twos:
        copy.wait_recv()
    totals = R2[0]
    for j in range(1, n_col):
        totals += R2[j]
    own = share // n_col
    totals = pltpu.roll(totals, (128 - own * c) % 128, 1)
    power = totals[0:4] / totals[4:8]
    pow_ref[...] = power[:, 0:own]
    R3[q] = jnp.broadcast_to(jnp.sum(power, axis=0, keepdims=True), (8, 128))
    threes = []
    for j in range(1, n_freq):
        copy = remote(R3.at[q], R3.at[q], r3_send.at[j], r3_recv.at[q], (r, c, (q + j) % n_freq))
        copy.start()
        threes.append(copy)
    for copy in twos:
        copy.wait_send()
    for j in range(1, n_freq):
        g = (q + j) % n_freq
        remote(R3.at[g], R3.at[g], r3_send.at[j], r3_recv.at[g], sib).wait_recv()
    surface = R3[0]
    for j in range(1, n_freq):
        surface += R3[j]
    surf_ref[...] = surface[0:1, 0:own] / total_freqs
    for copy in threes:
        copy.wait_send()


def solution(mesh):
    n_row, n_col, n_freq = (mesh.shape[a] for a in ("row", "col", "freq"))
    hbm = pl.BlockSpec(memory_space=pl.ANY)
    vmem = pl.BlockSpec(memory_space=pltpu.VMEM)

    def local(covariance, replica_table, slab_index):
        freqs, _, ch, table = replica_table.shape
        slab = slab_index.shape[0]
        own = slab // (n_row * n_col)
        sizes = (n_row, n_col, n_freq, ch, slab, table, freqs * n_freq)
        dma = pltpu.SemaphoreType.DMA
        power, surface = pl.pallas_call(
            functools.partial(kernel, sizes),
            out_shape=(jax.ShapeDtypeStruct((freqs, own), F32), jax.ShapeDtypeStruct((1, own), F32)),
            in_specs=[hbm, hbm, vmem],
            out_specs=(vmem, vmem),
            scratch_shapes=[
                pltpu.VMEM((freqs, 2, ch, table), BF16),
                pltpu.VMEM((freqs, 2 * ch, 2 * ch), BF16),
                pltpu.VMEM((freqs, 2 * ch, 2 * slab), BF16),
                pltpu.VMEM((table, slab), BF16),
                pltpu.VMEM((freqs, 2 * ch, 2 * slab), F32),
                pltpu.VMEM((3, ch, 2 * slab), BF16),
                pltpu.VMEM((freqs, ch, 2 * slab), BF16),
                pltpu.VMEM((freqs, 8, 2 * slab), F32),
                pltpu.VMEM((freqs, 8, slab), F32),
                pltpu.VMEM((n_row, 8, slab), F32),
                pltpu.VMEM((n_col, 8, 128), F32),
                pltpu.VMEM((n_freq, 8, 128), F32),
                dma((4,)), dma((4, 4)), dma((3, NCH)), dma((4, NCH)), dma, dma, dma, dma((4,)),
                dma((n_row,)), dma((n_row,)), dma((n_col,)), dma((n_col,)), dma((n_freq,)), dma((n_freq,)),
            ],
            compiler_params=pltpu.CompilerParams(
                collective_id=0, has_side_effects=True, vmem_limit_bytes=40 * 2**20),
        )(covariance, replica_table, slab_index.reshape(1, slab))
        return power, surface.reshape(own)

    in_specs = (P("freq", None, "row", "col"), P("freq", None, "col", None), P())
    out_specs = (P("freq", ("row", "col")), P(("row", "col")))
    return jax.shard_map(local, mesh=mesh, in_specs=in_specs, out_specs=out_specs, check_vma=False)
```

time: 733 us -> 84.4 us (0.12)
  blocking collectives: 559 us -> 0 us
  waiting for transfers between devices: 117 us -> 0 us
  Pallas kernels: 0 us -> 78.6 us
  between operations: 14.7 us -> 0.64 us
  other arithmetic: 13.9 us -> 0 us
  local copies, waits for them, and re-layouts: 15 us -> 4.96 us
    unnamed x1 -> x0, blocking collectives: 549 us -> none
    psum x1 -> x0, waiting for transfers between devices: 117 us -> none  [broadcast(): return lax.psum(jnp.where(mine, shard, jnp.zeros_like(shard)), axis)]
    pallas_call x0 -> x1, Pallas kernels: none -> 78.6 us  [local(): pl.pallas_call(functools.partial(kernel, sizes), out_shape=(jax.ShapeDtyp...]
    psum x1 -> x0, blocking collectives: 10.3 us -> none  [local(): surface = lax.psum(jnp.sum(power, axis=0), 'freq') / FREQ]
    reduce_sum x3 -> x0, other arithmetic: 7.5 us -> none  [the longest x1 5.19 us: local(): jnp.sum(row_slab[:, 0].astype(jnp.float32) * image_real + row_slab[:, 1]....]
  transfers between devices with their start and end apart: 1 -> 0, of which waited for: 1 -> 0; matrix products, arithmetic and copies ran while one was open for 1% -> 0% of each run, Pallas kernels for 0% -> 0%
where the time goes in v1:
time: 84.4 us; the launch traced here: 84.2 us
  Pallas kernels  78.6 us (93%)
  local copies, waits for them, and re-layouts  4.96 us (6%)
    pallas_call x1, Pallas kernels, local(): pl.pallas_call(functools.partial(kernel, sizes), out_shape=(jax.ShapeDtyp...  78.6 us
    unnamed x6, local copies, waits for them, and re-layouts  4.27 us

profile of v1, /device:TPU:1, one launch (start us, length us, event | category | flops | bytes accessed | tf_op | source)
XLA Modules:
  0.0 84.2 jit_solution(10296982412343471573)
XLA Ops:
  0.6 0.7 reshape.10.idx
  1.3 0.0 copy-start
  1.3 1.6 %copy-done = bf16[4,2,512,256]{3,2,1,0:T(8,128)(2,1)S(1)} copy-done((bf16[4,2,512,256]{3,2,1,0:T(8,128)(2,1)S(1)}, bf16[4,2,512,256]{3,2,1,0:T(8,128)(2,1)}, u32[]{:S(2)}) %copy-start) | copy-done | bytes 2097176
  2.9 0.0 copy-start.1
  2.9 1.6 %copy-done.1 = bf16[4,2,256,512]{3,2,1,0:T(8,128)(2,1)S(1)} copy-done((bf16[4,2,256,512]{3,2,1,0:T(8,128)(2,1)S(1)}, bf16[4,2,256,512]{3,2,1,0:T(8,128)(2,1)}, u32[]{:S(2)}) %copy-start.1) | copy-done | bytes 2097176
  4.5 78.6 %shard_map.50 = (f32[4,3]{1,0:T(4,128)S(1)}, f32[1,3]{1,0:T(1,128)S(1)}) custom-call(bf16[4,2,512,256]{3,2,1,0:T(8,128)(2,1)S(1)} %copy-done, bf16[4,2,256,512]{3,2,1,0:T(8,128)(2,1)S(1)} %copy-done.1, s32[1,384]{1,0:T(1,128)S(1)} %reshape.10.idx), custom_call_target="tpu_custom_call" | custom-call | tf_op jit(solution)/shard_map/pallas_call | solution.py:353
  83.1 0.6 copy.7
  83.7 0.5 copy.8
Async XLA Ops:
  1.3 1.6 %copy-start = (bf16[4,2,512,256]{3,2,1,0:T(8,128)(2,1)S(1)}, bf16[4,2,512,256]{3,2,1,0:T(8,128)(2,1)}, u32[]{:S(2)}) copy-start(bf16[4,2,512,256]{3,2,1,0:T(8,128)(2,1)} %cov.1) | copy-start | bytes 6291460
  2.9 1.6 %copy-start.1 = (bf16[4,2,256,512]{3,2,1,0:T(8,128)(2,1)S(1)}, bf16[4,2,256,512]{3,2,1,0:T(8,128)(2,1)}, u32[]{:S(2)}) copy-start(bf16[4,2,256,512]{3,2,1,0:T(8,128)(2,1)} %tbl.1) | copy-start | bytes 6291460

commit v2 on v1

--- a/solution.py
+++ b/solution.py
@@ -11,6 +11,8 @@
 F32 = jnp.float32
 BF16 = jnp.bfloat16
 NCH = 16
+LAG = 6
+SIB_LAG = 3
 
 
 def kernel(sizes, cov, tbl, idx, pow_ref, surf_ref,
@@ -29,6 +31,8 @@
     up = (r, (c + 2) % 16, q)
     down = (r, (c + 14) % 16, q)
     mate = ((r + 4) % 8, c, q)
+    up_mate = ((r + 4) % 8, (c + 2) % 16, q)
+    down_mate = ((r + 4) % 8, (c + 14) % 16, q)
     sib = (r, c + 1 - 2 * k, q)
 
     barrier = pltpu.get_barrier_semaphore()
@@ -38,6 +42,9 @@
         pl.semaphore_signal(barrier, inc=1, device_id=((r + j) % n_row, c, q), device_id_type=MESH)
     for j in range(1, n_freq):
         pl.semaphore_signal(barrier, inc=1, device_id=(r, c, (q + j) % n_freq), device_id_type=MESH)
+
+    for to in (up_mate, down_mate):
+        pl.semaphore_signal(barrier, inc=1, device_id=to, device_id_type=MESH)
 
     ends = (d == 0) | (d == 4)
     base = jnp.where(d >= 5, 2, 0)
@@ -96,8 +103,8 @@
     def send_down(src, j):
         return remote(src, B.at[to_down, chunk(j)], dn_send, b_recv.at[to_down, j], down)
 
-    def send_mate(src, j):
-        return remote(src, B.at[1, chunk(j)], z_send, b_recv.at[1, j], mate)
+    def send_mate(src, j, to=mate):
+        return remote(src, B.at[1, chunk(j)], z_send, b_recv.at[1, j], to)
 
     def send_sib(src, i, j):
         return remote(src, S.at[i, chunk(j)], s_send.at[i], s_recv.at[i, j], sib)
@@ -121,7 +128,7 @@
 
         @pl.when(i == 0)
         def _():
-            pl.semaphore_wait(barrier, n_col + n_row + n_freq - 3)
+            pl.semaphore_wait(barrier, n_col + n_row + n_freq - 1)
 
         @pl.when(ends & (i == 0))
         def _():
@@ -183,9 +190,11 @@
 
     @pl.when(d != 0)
     def _():
-        lag_p = jnp.where(d <= 4, d, d - 4) - 1
-        lag_m = jnp.where(d >= 4, 8 - d, 4 - d) - 1
-        lag_1 = jnp.where(d == 4, 4, hops + 1)
+        lag_p = (jnp.where(d <= 4, d, d - 4) - 1) * LAG
+        lag_m = (jnp.where(d >= 4, 8 - d, 4 - d) - 1) * LAG
+        lag_z = jnp.where(hops == 3, 2 * LAG + 2, hops * LAG)
+        lag_0 = (hops - 1) * LAG + SIB_LAG
+        lag_1 = jnp.where(d == 4, 3 * LAG, lag_z) + SIB_LAG
 
         def within(j):
             return (j >= 0) & (j < NCH)
@@ -193,12 +202,12 @@
         def step(t, carry):
             jp = t - lag_p
 
-            @pl.when(within(jp))
+            @pl.when(within(jp) & (d != 7))
             def _():
                 wait_in(from_down, jp)
                 here = B.at[from_down, chunk(jp)]
 
-                @pl.when((d != 4) & (d != 7))
+                @pl.when((d != 4) & (d != 6))
                 def _():
                     send_up(here, jp).start()
 
@@ -210,14 +219,18 @@
                 def _():
                     send_mate(here, jp).start()
 
+                @pl.when(d == 6)
+                def _():
+                    send_mate(here, jp, up_mate).start()
+
             jm = t - lag_m
 
-            @pl.when(within(jm))
+            @pl.when(within(jm) & (d != 1))
             def _():
                 wait_in(from_up, jm)
                 here = B.at[from_up, chunk(jm)]
 
-                @pl.when((d != 4) & (d != 1))
+                @pl.when((d != 4) & (d != 2))
                 def _():
                     send_down(here, jm).start()
 
@@ -229,14 +242,18 @@
                 def _():
                     send_mate(here, jm).start()
 
-            jz = t - hops
+                @pl.when(d == 2)
+                def _():
+                    send_mate(here, jm, down_mate).start()
+
+            jz = t - lag_z
 
             @pl.when(within(jz) & (d != 4))
             def _():
                 wait_in(1, jz)
                 send_sib(B.at[1, chunk(jz)], 1, jz).start()
 
-            j0 = t - hops
+            j0 = t - lag_0
 
             @pl.when(within(j0))
             def _():
@@ -252,7 +269,7 @@
 
             return carry
 
-        lax.fori_loop(0, NCH + 4, step, 0)
+        lax.fori_loop(0, NCH + lag_1, step, 0)
 
     scale = jnp.where(d == 0, 1.0, 2.0).astype(F32)
     rows8 = lax.broadcasted_iota(jnp.int32, (8, slab), 0)
@@ -278,15 +295,19 @@
 
     whole = S.at[0]
 
-    @pl.when((d != 4) & (d != 7) | ends)
+    @pl.when((d != 6) & (d != 7))
     def _():
         sent(whole, up_send)
 
-    @pl.when((d != 4) & (d != 1) | ends)
+    @pl.when((d != 2) & (d != 1))
     def _():
         sent(whole, dn_send)
 
-    @pl.when(~ends)
+    @pl.when((d == 2) | (d == 3) | (d == 5) | (d == 6))
+    def _():
+        sent(whole, z_send)
+
+    @pl.when((d == 2) | (d == 6))
     def _():
         sent(whole, z_send)
 
@@ -341,7 +362,7 @@
 
 def solution(mesh):
     n_row, n_col, n_freq = (mesh.shape[a] for a in ("row", "col", "freq"))
-    hbm = pl.BlockSpec(memory_space=pl.ANY)
+    hbm = pl.BlockSpec(memory_space=pltpu.HBM)
     vmem = pl.BlockSpec(memory_space=pltpu.VMEM)
 
     def local(covariance, replica_table, slab_index):
@@ -372,7 +393,7 @@
                 dma((n_row,)), dma((n_row,)), dma((n_col,)), dma((n_col,)), dma((n_freq,)), dma((n_freq,)),
             ],
             compiler_params=pltpu.CompilerParams(
-                collective_id=0, has_side_effects=True, vmem_limit_bytes=40 * 2**20),
+                collective_id=0, has_side_effects=True, vmem_limit_bytes=63 * 2**20),
         )(covariance, replica_table, slab_index.reshape(1, slab))
         return power, surface.reshape(own)
 

time: 84.4 us -> 55.1 us (0.65)
  Pallas kernels: 78.6 us -> 50.6 us
  local copies, waits for them, and re-layouts: 4.96 us -> 3.63 us
    pallas_call x1, Pallas kernels: 78.6 us -> 50.6 us  [local(): pl.pallas_call(functools.partial(kernel, sizes), out_shape=(jax.ShapeDtyp...]
    unnamed x6 -> x2, local copies, waits for them, and re-layouts: 4.27 us -> 2.39 us
where the time goes in v2:
time: 55.1 us; the launch traced here: 54.9 us
  Pallas kernels  50.6 us (92%)
  local copies, waits for them, and re-layouts  3.63 us (7%)
  between operations  0.64 us (1%)
    pallas_call x1, Pallas kernels, local(): pl.pallas_call(functools.partial(kernel, sizes), out_shape=(jax.ShapeDtyp...  50.6 us
    unnamed x2, local copies, waits for them, and re-layouts  2.39 us
    reshape x1, local copies, waits for them, and re-layouts, local(): slab_index.reshape(1, slab)  1.25 us

profile of v2, /device:TPU:1, one launch (start us, length us, event | category | flops | bytes accessed | tf_op | source)
XLA Modules:
  0.0 54.9 jit_solution(6427917825627252051)
XLA Ops:
  0.6 1.2 %reshape.10.idx = s32[1,384]{1,0:T(1,128)} reshape(s32[384]{0:T(512)} %param.5) | data formatting | bytes 3072 | tf_op jit(solution)/shard_map/reshape | solution.py:397
  1.9 50.6 %shard_map.50 = (f32[4,3]{1,0:T(4,128)}, f32[1,3]{1,0:T(1,128)}) custom-call(bf16[4,2,512,256]{3,2,1,0:T(8,128)(2,1)} %cov.1, bf16[4,2,256,512]{3,2,1,0:T(8,128)(2,1)} %tbl.1, s32[1,384]{1,0:T(1,128)} %reshape.10.idx), custom_call_target="tpu_custom_call" | custom-call | tf_op jit(solution)/shard_map/pallas_call | solution.py:374
  52.5 1.2 %copy.7 = f32[4,3]{1,0:T(4,128)} copy(f32[4,3]{1,0:T(4,128)} %get-tuple-element.8) | data formatting | bytes 96
  53.8 1.1 %copy.8 = f32[3]{0:T(128)} copy(f32[3]{0:T(128)} %bitcast.1) | data formatting | bytes 24

commit v3 on v2

v3 whole, which is shorter than its diff:
```python
import functools

import jax
import jax.numpy as jnp
from jax import lax
from jax.experimental import pallas as pl
from jax.experimental.pallas import tpu as pltpu
from jax.sharding import PartitionSpec as P

MESH = pl.DeviceIdType.MESH
F32 = jnp.float32
BF16 = jnp.bfloat16
NCH = 16
LAG = 6
SIB_LAG = 3
GREET = 6
ROUNDS = 5


def kernel(sizes, cov, tbl, idx, pow_ref, surf_ref,
           T, C, X, OH, IM, B, S, ACC, WT, A0, R0, A1, R1, A2, R2,
           tsem, csem, b_recv, s_recv, up_send, dn_send, z_send, s_send,
           a0_send, a0_recv, a1_send, a1_recv, a2_send, a2_recv, gossip):
    n_row, n_col, n_freq, ch, slab, table, total_freqs = sizes
    cr = ch // NCH
    r = lax.axis_index("row")
    c = lax.axis_index("col")
    q = lax.axis_index("freq")
    x = r % 4
    y = c // 2
    k = c % 2
    zl = r // 4
    z = 2 * q + zl
    d = (y - r + 8) % 8
    up = (r, (c + 2) % 16, q)
    down = (r, (c + 14) % 16, q)
    mate = ((r + 4) % 8, c, q)
    up_mate = ((r + 4) % 8, (c + 2) % 16, q)
    down_mate = ((r + 4) % 8, (c + 14) % 16, q)
    sib = (r, c + 1 - 2 * k, q)
    z_up, z_down = (z + 1) % 8, (z + 7) % 8
    near = [
        up, down, sib,
        (zl * 4 + (x + 1) % 4, c, q), (zl * 4 + (x + 3) % 4, c, q),
        ((z_up % 2) * 4 + x, c, z_up // 2), ((z_down % 2) * 4 + x, c, z_down // 2),
    ]

    barrier = pltpu.get_barrier_semaphore()
    greeted = near + [up_mate, down_mate]
    for to in greeted:
        pl.semaphore_signal(barrier, inc=1, device_id=to, device_id_type=MESH)

    ends = (d == 0) | (d == 4)
    base = jnp.where(d >= 5, 2, 0)
    n_slots = jnp.where(d == 0, 4, 2)

    def freq_of(i):
        first = jnp.where(i == 0, base + zl, jnp.where(ends, 2 + zl, base + 1 - zl))
        low, high = jnp.where(ends, 1 - zl, 2 - base + zl), jnp.where(ends, 3 - zl, 3 - base - zl)
        return jnp.where(i < 2, first, jnp.where(i == 2, low, high))

    def table_copy(i):
        return pltpu.make_async_copy(tbl.at[freq_of(i)], T.at[i], tsem.at[i])

    def cov_copies(i):
        out = []
        for part in range(2):
            for half in range(2):
                rows = pl.ds(pl.multiple_of((k if half == 0 else 1 - k) * ch, ch), ch)
                out.append(pltpu.make_async_copy(
                    cov.at[freq_of(i), part, rows, :],
                    C.at[i, pl.ds(half * ch, ch), pl.ds(part * ch, ch)],
                    csem.at[i, 2 * part + half]))
        return out

    def start_table(i, carry):
        table_copy(i).start()
        return carry

    def start_cov(i, carry):
        for copy in cov_copies(i):
            copy.start()
        return carry

    lax.fori_loop(0, 4, start_table, 0)
    lax.fori_loop(0, n_slots, start_cov, 0)

    share = slab // n_row
    own = share // n_col
    points = lax.broadcasted_iota(jnp.int32, (table, slab), 0)
    taken = jnp.where(points == idx[...], 1.0, 0.0).astype(BF16)
    lane = lax.broadcasted_iota(jnp.int32, (slab, slab), 1)
    source = lane % n_row * share + lane % 128 // n_row * own + lane // 128
    order = jnp.where(lax.broadcasted_iota(jnp.int32, (slab, slab), 0) == source, 1.0, 0.0).astype(BF16)
    OH[...] = jnp.dot(taken, order, preferred_element_type=F32).astype(BF16)
    ACC[...] = jnp.zeros_like(ACC)
    A0[...] = jnp.zeros_like(A0)
    A1[...] = jnp.zeros_like(A1)

    def chunk(j):
        return pl.ds(pl.multiple_of(j * cr, cr), cr)

    def remote(src, dst, send, recv, to):
        return pltpu.make_async_remote_copy(
            src_ref=src, dst_ref=dst, send_sem=send, recv_sem=recv, device_id=to, device_id_type=MESH)

    to_up = jnp.where(d <= 3, 0, 2)
    to_down = jnp.where((d == 0) | (d >= 6), 0, jnp.where(d == 5, 1, 2))
    from_down = jnp.where(d <= 4, 0, 2)
    from_up = jnp.where(d >= 5, 0, jnp.where(d == 4, 1, 2))

    def send_up(src, j):
        return remote(src, B.at[to_up, chunk(j)], up_send, b_recv.at[to_up, j], up)

    def send_down(src, j):
        return remote(src, B.at[to_down, chunk(j)], dn_send, b_recv.at[to_down, j], down)

    def send_mate(src, j, to=mate):
        return remote(src, B.at[1, chunk(j)], z_send, b_recv.at[1, j], to)

    def send_sib(src, i, j):
        return remote(src, S.at[i, chunk(j)], s_send.at[i], s_recv.at[i, j], sib)

    def own_rows(i, j):
        return X.at[i, chunk(j), :]

    def gather(i, carry):
        table_copy(i).wait()
        both = jnp.dot(T[i].reshape(2 * ch, table), OH[...], preferred_element_type=F32)
        a, b = both[:ch], both[ch:]
        na, nb = a.astype(BF16), b.astype(BF16)
        X[i, 0:ch, 0:slab] = na
        X[i, 0:ch, slab:2 * slab] = nb
        X[i, ch:2 * ch, 0:slab] = -nb
        X[i, ch:2 * ch, slab:2 * slab] = na

        WT[i] = jnp.sum((a * a + b * b).reshape(ch // 8, 8, slab), axis=0)

        @pl.when(i == 0)
        def _():
            pl.semaphore_wait(barrier, len(greeted))

        @pl.when(ends & (i == 0))
        def _():
            def go(j, carry):
                send_up(own_rows(i, j), j).start()
                return carry
            lax.fori_loop(0, NCH, go, 0)

        @pl.when(ends & (i == 1))
        def _():
            def go(j, carry):
                send_down(own_rows(i, j), j).start()
                return carry
            lax.fori_loop(0, NCH, go, 0)

        @pl.when(d == 0)
        def _():
            def go(j, carry):
                send_sib(own_rows(i, j), i, j).start()
                return carry
            lax.fori_loop(0, NCH, go, 0)

        return carry

    lax.fori_loop(0, 4, gather, 0)

    def image(i, carry):
        for copy in cov_copies(i):
            copy.wait()
        IM[i] = jnp.dot(C[i], X[i], preferred_element_type=F32)
        return carry

    lax.fori_loop(0, n_slots, image, 0)

    def wait_in(slot, j):
        remote(B.at[slot, chunk(j)], B.at[slot, chunk(j)], z_send, b_recv.at[slot, j], sib).wait_recv()

    def wait_sib(i, j):
        remote(S.at[i, chunk(j)], S.at[i, chunk(j)], z_send, s_recv.at[i, j], sib).wait_recv()

    def fold(w, im):
        return jnp.sum((w.astype(F32) * im).reshape(cr // 8, 8, 2 * slab), axis=0)

    def combine(own, i, j):
        mine = fold(own[...], IM[i, chunk(j), :])
        other = pl.ds(pl.multiple_of(ch + j * cr, cr), cr)
        ACC[i] += mine + fold(S[i, chunk(j), :], IM[i, other, :])

    def tiles(to, sums):
        lines = lax.broadcasted_iota(jnp.int32, (16, 128), 0)
        part = jnp.zeros((16, 128), F32)
        for i in range(4):
            total = jnp.sum(sums(i), axis=0, keepdims=True)
            for m in range(own):
                part = jnp.where(lines == own * freq_of(i) + m, total[:, 128 * m:128 * (m + 1)], part)
        to[:, :, 0:16] = part.T.reshape(n_col, n_row, 16)

    def to_column(src, dst, send, recv):
        def go(j, carry):
            to = (c + j) % n_col
            remote(src.at[to], dst.at[j], send, recv, (r, to, q)).start()
            return carry
        lax.fori_loop(1, n_col, go, 0)

    def column_wait(dst, send, recv):
        others = dst.at[pl.ds(1, n_col - 1)]
        return remote(others, others, send, recv, sib)

    def greet(n):
        for to in near:
            pl.semaphore_signal(gossip.at[n], inc=1, device_id=to, device_id_type=MESH)

    tiles(A0, lambda i: WT[i])

    hops = jnp.where(d <= 4, d, 8 - d)

    lag_p = (jnp.where(d <= 4, d, d - 4) - 1) * LAG
    lag_m = (jnp.where(d >= 4, 8 - d, 4 - d) - 1) * LAG
    lag_z = jnp.where(hops == 3, 2 * LAG + 2, hops * LAG)
    lag_0 = (hops - 1) * LAG + SIB_LAG
    lag_1 = jnp.where(d == 4, 3 * LAG, lag_z) + SIB_LAG
    off = d != 0

    def within(j):
        return (j >= 0) & (j < NCH)

    def step(t, carry):
        jp = t - lag_p

        @pl.when(off & within(jp) & (d != 7))
        def _():
            wait_in(from_down, jp)
            here = B.at[from_down, chunk(jp)]

            @pl.when((d != 4) & (d != 6))
            def _():
                send_up(here, jp).start()

            @pl.when(d <= 4)
            def _():
                send_sib(here, 0, jp).start()

            @pl.when(d >= 5)
            def _():
                send_mate(here, jp).start()

            @pl.when(d == 6)
            def _():
                send_mate(here, jp, up_mate).start()

        jm = t - lag_m

        @pl.when(off & within(jm) & (d != 1))
        def _():
            wait_in(from_up, jm)
            here = B.at[from_up, chunk(jm)]

            @pl.when((d != 4) & (d != 2))
            def _():
                send_down(here, jm).start()

            @pl.when(d >= 4)
            def _():
                send_sib(here, from_up, jm).start()

            @pl.when(d <= 3)
            def _():
                send_mate(here, jm).start()

            @pl.when(d == 2)
            def _():
                send_mate(here, jm, down_mate).start()

        jz = t - lag_z

        @pl.when(off & within(jz) & (d != 4))
        def _():
            wait_in(1, jz)
            send_sib(B.at[1, chunk(jz)], 1, jz).start()

        j0 = t - lag_0

        @pl.when(off & within(j0))
        def _():
            wait_sib(0, j0)
            combine(B.at[0, chunk(j0)], 0, j0)

        j1 = t - lag_1

        @pl.when(off & within(j1))
        def _():
            wait_sib(1, j1)
            combine(B.at[1, chunk(j1)], 1, j1)

        js = t - GREET

        @pl.when((d == 0) & within(js))
        def _():
            for i in range(4):
                wait_sib(i, js)
                combine(own_rows(i, js), i, js)

        @pl.when((t % GREET == 0) & (t <= ROUNDS * GREET))
        def _():
            n = t // GREET

            @pl.when(n > 0)
            def _():
                pl.semaphore_wait(gossip.at[n - 1], len(near))

            @pl.when(n < ROUNDS)
            def _():
                greet(n)

            @pl.when(n == ROUNDS - 1)
            def _():
                to_column(A0, R0, a0_send, a0_recv)

        return carry

    lax.fori_loop(0, NCH + 3 * LAG + SIB_LAG + 1, step, 0)

    scale = jnp.where(d == 0, 1.0, 2.0).astype(F32)
    tiles(A1, lambda i: (ACC[i, :, 0:slab] + ACC[i, :, slab:2 * slab]) * scale)
    to_column(A1, R1, a1_send, a1_recv)
    column_wait(R0, a0_send, a0_recv).wait()
    norm = A0[c]
    for j in range(1, n_col):
        norm += R0[j]
    lanes = lax.broadcasted_iota(jnp.int32, (8, 128), 1)
    used = lanes < 4 * own
    norm = jnp.where(used, norm, 1.0)

    def sent(ref, sem):
        remote(ref, ref, sem, b_recv.at[0, 0], sib).wait_send()

    whole = S.at[0]

    @pl.when((d != 6) & (d != 7))
    def _():
        sent(whole, up_send)

    @pl.when((d != 2) & (d != 1))
    def _():
        sent(whole, dn_send)

    @pl.when((d == 2) | (d == 3) | (d == 5) | (d == 6))
    def _():
        sent(whole, z_send)

    @pl.when((d == 2) | (d == 6))
    def _():
        sent(whole, z_send)

    def sib_sent(i, carry):
        sent(whole, s_send.at[i])
        return carry

    lax.fori_loop(0, n_slots, sib_sent, 0)

    column_wait(R1, a1_send, a1_recv).wait()
    form = A1[c]
    for j in range(1, n_col):
        form += R1[j]
    power = jnp.where(used, form / norm, 0.0)
    total = power
    for f in range(1, 4):
        total += pltpu.roll(power, 128 - own * f, 1)
    both = jnp.where(used, power, pltpu.roll(total, 64, 1))
    for j in range(n_row):
        A2[j] = both[j:j + 1]
    me = q * n_row + r
    R2[me] = A2[r]

    def go(j, carry):
        to, at = (r + j) % n_row, (q + j // n_row) % n_freq
        remote(A2.at[to], R2.at[me], a2_send, a2_recv, (to, c, at)).start()
        return carry

    lax.fori_loop(1, n_row * n_freq, go, 0)
    others = R2.at[pl.ds(1, n_row * n_freq - 1)]
    remote(others, others, a2_send, a2_recv, sib).wait()
    whole_power = R2[q * n_row]
    for j in range(1, n_row):
        whole_power += R2[q * n_row + j]
    surface = R2[0]
    for j in range(1, n_row * n_freq):
        surface += R2[j]
    line = lax.broadcasted_iota(jnp.int32, (4, 128), 0)
    out = jnp.broadcast_to(whole_power, (4, 128))
    for f in range(1, 4):
        out = jnp.where(line == f, pltpu.roll(whole_power, 128 - own * f, 1), out)
    pow_ref[...] = out[:, 0:own]
    surf_ref[...] = pltpu.roll(surface, 64, 1)[:, 0:own] / total_freqs


def solution(mesh):
    n_row, n_col, n_freq = (mesh.shape[a] for a in ("row", "col", "freq"))
    hbm = pl.BlockSpec(memory_space=pltpu.HBM)
    vmem = pl.BlockSpec(memory_space=pltpu.VMEM)

    def local(covariance, replica_table, slab_index):
        freqs, _, ch, table = replica_table.shape
        slab = slab_index.shape[0]
        own = slab // (n_row * n_col)
        sizes = (n_row, n_col, n_freq, ch, slab, table, freqs * n_freq)
        dma = pltpu.SemaphoreType.DMA
        power, surface = pl.pallas_call(
            functools.partial(kernel, sizes),
            out_shape=(jax.ShapeDtypeStruct((freqs, own), F32), jax.ShapeDtypeStruct((1, own), F32)),
            in_specs=[hbm, hbm, vmem],
            out_specs=(vmem, vmem),
            scratch_shapes=[
                pltpu.VMEM((freqs, 2, ch, table), BF16),
                pltpu.VMEM((freqs, 2 * ch, 2 * ch), BF16),
                pltpu.VMEM((freqs, 2 * ch, 2 * slab), BF16),
                pltpu.VMEM((table, slab), BF16),
                pltpu.VMEM((freqs, 2 * ch, 2 * slab), F32),
                pltpu.VMEM((3, ch, 2 * slab), BF16),
                pltpu.VMEM((freqs, ch, 2 * slab), BF16),
                pltpu.VMEM((freqs, 8, 2 * slab), F32),
                pltpu.VMEM((freqs, 8, slab), F32),
                pltpu.VMEM((n_col, n_row, 128), F32),
                pltpu.VMEM((n_col, n_row, 128), F32),
                pltpu.VMEM((n_col, n_row, 128), F32),
                pltpu.VMEM((n_col, n_row, 128), F32),
                pltpu.VMEM((n_row, 1, 128), F32),
                pltpu.VMEM((n_row * n_freq, 1, 128), F32),
                dma((4,)), dma((4, 4)), dma((3, NCH)), dma((4, NCH)), dma, dma, dma, dma((4,)),
                dma, dma, dma, dma, dma, dma, pltpu.SemaphoreType.REGULAR((ROUNDS,)),
            ],
            compiler_params=pltpu.CompilerParams(
                collective_id=0, has_side_effects=True, vmem_limit_bytes=63 * 2**20),
        )(covariance, replica_table, slab_index.reshape(1, slab))
        return power, surface.reshape(own)

    in_specs = (P("freq", None, "row", "col"), P("freq", None, "col", None), P())
    out_specs = (P("freq", ("row", "col")), P(("row", "col")))
    return jax.shard_map(local, mesh=mesh, in_specs=in_specs, out_specs=out_specs, check_vma=False)
```

time: 55.1 us -> 53.8 us (0.976)
  Pallas kernels: 50.6 us -> 49.3 us
    pallas_call x1, Pallas kernels: 50.6 us -> 49.3 us  [local(): pl.pallas_call(functools.partial(kernel, sizes), out_shape=(jax.ShapeDtyp...]
where the time goes in v3:
time: 53.8 us; the launch traced here: 53.6 us
  Pallas kernels  49.3 us (92%)
  local copies, waits for them, and re-layouts  3.63 us (7%)
  between operations  0.64 us (1%)
    pallas_call x1, Pallas kernels, local(): pl.pallas_call(functools.partial(kernel, sizes), out_shape=(jax.ShapeDtyp...  49.3 us
    unnamed x2, local copies, waits for them, and re-layouts  2.39 us
    reshape x1, local copies, waits for them, and re-layouts, local(): slab_index.reshape(1, slab)  1.25 us

profile of v3, /device:TPU:1, one launch (start us, length us, event | category | flops | bytes accessed | tf_op | source)
XLA Modules:
  0.0 53.6 jit_solution(7197319984241571917)
XLA Ops:
  0.6 1.2 %reshape.10.idx = s32[1,384]{1,0:T(1,128)} reshape(s32[384]{0:T(512)} %param.5) | data formatting | bytes 3072 | tf_op jit(solution)/shard_map/reshape | solution.py:435
  1.9 49.3 %shard_map.50 = (f32[4,3]{1,0:T(4,128)}, f32[1,3]{1,0:T(1,128)}) custom-call(bf16[4,2,512,256]{3,2,1,0:T(8,128)(2,1)} %cov.1, bf16[4,2,256,512]{3,2,1,0:T(8,128)(2,1)} %tbl.1, s32[1,384]{1,0:T(1,128)} %reshape.10.idx), custom_call_target="tpu_custom_call" | custom-call | tf_op jit(solution)/shard_map/pallas_call | solution.py:409
  51.2 1.2 %copy.7 = f32[4,3]{1,0:T(4,128)} copy(f32[4,3]{1,0:T(4,128)} %get-tuple-element.8) | data formatting | bytes 96
  52.5 1.1 %copy.8 = f32[3]{0:T(128)} copy(f32[3]{0:T(128)} %bitcast.1) | data formatting | bytes 24

commit v4 on v3

--- a/solution.py
+++ b/solution.py
@@ -12,13 +12,13 @@
 BF16 = jnp.bfloat16
 NCH = 16
 LAG = 6
-SIB_LAG = 3
-GREET = 6
-ROUNDS = 5
+MIN_LAG = 8
+GREET = 10
+ROUNDS = 3
 
 
 def kernel(sizes, cov, tbl, idx, pow_ref, surf_ref,
-           T, C, X, OH, IM, B, S, ACC, WT, A0, R0, A1, R1, A2, R2,
+           T, C, X, OH, IM, SI, B, ACC, WT, A0, R0, A1, R1, A2, R2,
            tsem, csem, b_recv, s_recv, up_send, dn_send, z_send, s_send,
            a0_send, a0_recv, a1_send, a1_recv, a2_send, a2_recv, gossip):
     n_row, n_col, n_freq, ch, slab, table, total_freqs = sizes
@@ -26,11 +26,9 @@
     r = lax.axis_index("row")
     c = lax.axis_index("col")
     q = lax.axis_index("freq")
-    x = r % 4
     y = c // 2
     k = c % 2
     zl = r // 4
-    z = 2 * q + zl
     d = (y - r + 8) % 8
     up = (r, (c + 2) % 16, q)
     down = (r, (c + 14) % 16, q)
@@ -38,15 +36,13 @@
     up_mate = ((r + 4) % 8, (c + 2) % 16, q)
     down_mate = ((r + 4) % 8, (c + 14) % 16, q)
     sib = (r, c + 1 - 2 * k, q)
-    z_up, z_down = (z + 1) % 8, (z + 7) % 8
-    near = [
-        up, down, sib,
-        (zl * 4 + (x + 1) % 4, c, q), (zl * 4 + (x + 3) % 4, c, q),
-        ((z_up % 2) * 4 + x, c, z_up // 2), ((z_down % 2) * 4 + x, c, z_down // 2),
-    ]
+    across = ((r + 4) % 8, c, (q + jnp.where(zl == 1, 1, n_freq - 1)) % n_freq)
+    column = [(r, (c + j) % n_col, q) for j in range(1, n_col)]
+    rows = [((r + j) % n_row, c, q) for j in range(1, n_row)]
+    near = rows + [across]
 
     barrier = pltpu.get_barrier_semaphore()
-    greeted = near + [up_mate, down_mate]
+    greeted = column + near + [up_mate, down_mate]
     for to in greeted:
         pl.semaphore_signal(barrier, inc=1, device_id=to, device_id_type=MESH)
 
@@ -88,14 +84,12 @@
     share = slab // n_row
     own = share // n_col
     points = lax.broadcasted_iota(jnp.int32, (table, slab), 0)
-    taken = jnp.where(points == idx[...], 1.0, 0.0).astype(BF16)
+    taken = jnp.where(points == idx[...].reshape(1, slab), 1.0, 0.0).astype(BF16)
     lane = lax.broadcasted_iota(jnp.int32, (slab, slab), 1)
     source = lane % n_row * share + lane % 128 // n_row * own + lane // 128
     order = jnp.where(lax.broadcasted_iota(jnp.int32, (slab, slab), 0) == source, 1.0, 0.0).astype(BF16)
     OH[...] = jnp.dot(taken, order, preferred_element_type=F32).astype(BF16)
     ACC[...] = jnp.zeros_like(ACC)
-    A0[...] = jnp.zeros_like(A0)
-    A1[...] = jnp.zeros_like(A1)
 
     def chunk(j):
         return pl.ds(pl.multiple_of(j * cr, cr), cr)
@@ -118,8 +112,8 @@
     def send_mate(src, j, to=mate):
         return remote(src, B.at[1, chunk(j)], z_send, b_recv.at[1, j], to)
 
-    def send_sib(src, i, j):
-        return remote(src, S.at[i, chunk(j)], s_send.at[i], s_recv.at[i, j], sib)
+    def send_image(i):
+        return remote(IM.at[i, pl.ds(ch, ch)], SI.at[i], s_send.at[i], s_recv.at[i], sib)
 
     def own_rows(i, j):
         return X.at[i, chunk(j), :]
@@ -154,13 +148,6 @@
                 return carry
             lax.fori_loop(0, NCH, go, 0)
 
-        @pl.when(d == 0)
-        def _():
-            def go(j, carry):
-                send_sib(own_rows(i, j), i, j).start()
-                return carry
-            lax.fori_loop(0, NCH, go, 0)
-
         return carry
 
     lax.fori_loop(0, 4, gather, 0)
@@ -169,32 +156,36 @@
         for copy in cov_copies(i):
             copy.wait()
         IM[i] = jnp.dot(C[i], X[i], preferred_element_type=F32)
-        return carry
-
-    lax.fori_loop(0, n_slots, image, 0)
+        send_image(i).start()
+        return carry
 
     def wait_in(slot, j):
         remote(B.at[slot, chunk(j)], B.at[slot, chunk(j)], z_send, b_recv.at[slot, j], sib).wait_recv()
 
-    def wait_sib(i, j):
-        remote(S.at[i, chunk(j)], S.at[i, chunk(j)], z_send, s_recv.at[i, j], sib).wait_recv()
-
     def fold(w, im):
         return jnp.sum((w.astype(F32) * im).reshape(cr // 8, 8, 2 * slab), axis=0)
 
-    def combine(own, i, j):
-        mine = fold(own[...], IM[i, chunk(j), :])
-        other = pl.ds(pl.multiple_of(ch + j * cr, cr), cr)
-        ACC[i] += mine + fold(S[i, chunk(j), :], IM[i, other, :])
-
-    def tiles(to, sums):
-        lines = lax.broadcasted_iota(jnp.int32, (16, 128), 0)
-        part = jnp.zeros((16, 128), F32)
+    def combine(replicas, i, j):
+        @pl.when(j == 0)
+        def _():
+            send_image(i).wait_recv()
+
+        total = IM[i, chunk(j), :] + SI[i, chunk(j), :]
+        ACC[i] += fold(replicas[...], total)
+
+    def lines(to, sums):
+        line = lax.broadcasted_iota(jnp.int32, (n_col, 128), 0)
+        group = lax.broadcasted_iota(jnp.int32, (n_col, 128), 1) // n_row
+        out = jnp.zeros((n_col, 128), F32)
         for i in range(4):
             total = jnp.sum(sums(i), axis=0, keepdims=True)
             for m in range(own):
-                part = jnp.where(lines == own * freq_of(i) + m, total[:, 128 * m:128 * (m + 1)], part)
-        to[:, :, 0:16] = part.T.reshape(n_col, n_row, 16)
+                kept = jnp.where(line == group, total[:, 128 * m:128 * (m + 1)], 0.0)
+                for shift in (8, 16, 32, 64):
+                    kept += pltpu.roll(kept, shift, 1)
+                out = jnp.where(group == own * freq_of(i) + m, kept, out)
+        for j in range(n_col):
+            to[j] = out[j:j + 1]
 
     def to_column(src, dst, send, recv):
         def go(j, carry):
@@ -211,15 +202,18 @@
         for to in near:
             pl.semaphore_signal(gossip.at[n], inc=1, device_id=to, device_id_type=MESH)
 
-    tiles(A0, lambda i: WT[i])
+    lax.fori_loop(0, n_slots, image, 0)
+    lines(A0, lambda i: WT[i])
+    to_column(A0, R0, a0_send, a0_recv)
+    greet(0)
 
     hops = jnp.where(d <= 4, d, 8 - d)
 
     lag_p = (jnp.where(d <= 4, d, d - 4) - 1) * LAG
     lag_m = (jnp.where(d >= 4, 8 - d, 4 - d) - 1) * LAG
     lag_z = jnp.where(hops == 3, 2 * LAG + 2, hops * LAG)
-    lag_0 = (hops - 1) * LAG + SIB_LAG
-    lag_1 = jnp.where(d == 4, 3 * LAG, lag_z) + SIB_LAG
+    lag_0 = jnp.maximum((hops - 1) * LAG, MIN_LAG)
+    lag_1 = jnp.maximum(jnp.where(d == 4, 3 * LAG, lag_z), MIN_LAG)
     off = d != 0
 
     def within(j):
@@ -237,10 +231,6 @@
             def _():
                 send_up(here, jp).start()
 
-            @pl.when(d <= 4)
-            def _():
-                send_sib(here, 0, jp).start()
-
             @pl.when(d >= 5)
             def _():
                 send_mate(here, jp).start()
@@ -260,10 +250,6 @@
             def _():
                 send_down(here, jm).start()
 
-            @pl.when(d >= 4)
-            def _():
-                send_sib(here, from_up, jm).start()
-
             @pl.when(d <= 3)
             def _():
                 send_mate(here, jm).start()
@@ -277,65 +263,53 @@
         @pl.when(off & within(jz) & (d != 4))
         def _():
             wait_in(1, jz)
-            send_sib(B.at[1, chunk(jz)], 1, jz).start()
 
         j0 = t - lag_0
 
         @pl.when(off & within(j0))
         def _():
-            wait_sib(0, j0)
             combine(B.at[0, chunk(j0)], 0, j0)
 
         j1 = t - lag_1
 
         @pl.when(off & within(j1))
         def _():
-            wait_sib(1, j1)
             combine(B.at[1, chunk(j1)], 1, j1)
 
-        js = t - GREET
+        js = t - MIN_LAG
 
         @pl.when((d == 0) & within(js))
         def _():
-            for i in range(4):
-                wait_sib(i, js)
+            def each(i, carry):
                 combine(own_rows(i, js), i, js)
-
-        @pl.when((t % GREET == 0) & (t <= ROUNDS * GREET))
-        def _():
-            n = t // GREET
-
-            @pl.when(n > 0)
+                return carry
+            lax.fori_loop(0, 4, each, 0)
+
+        for n in range(1, ROUNDS):
+            @pl.when(t == n * GREET)
             def _():
                 pl.semaphore_wait(gossip.at[n - 1], len(near))
-
-            @pl.when(n < ROUNDS)
-            def _():
                 greet(n)
 
-            @pl.when(n == ROUNDS - 1)
-            def _():
-                to_column(A0, R0, a0_send, a0_recv)
-
-        return carry
-
-    lax.fori_loop(0, NCH + 3 * LAG + SIB_LAG + 1, step, 0)
+        return carry
+
+    steps = jnp.where(d == 0, MIN_LAG, jnp.maximum(lag_0, lag_1))
+    lax.fori_loop(0, NCH + jnp.maximum(steps, (ROUNDS - 1) * GREET + 1 - NCH), step, 0)
 
     scale = jnp.where(d == 0, 1.0, 2.0).astype(F32)
-    tiles(A1, lambda i: (ACC[i, :, 0:slab] + ACC[i, :, slab:2 * slab]) * scale)
+    lines(A1, lambda i: (ACC[i, :, 0:slab] + ACC[i, :, slab:2 * slab]) * scale)
     to_column(A1, R1, a1_send, a1_recv)
     column_wait(R0, a0_send, a0_recv).wait()
     norm = A0[c]
     for j in range(1, n_col):
         norm += R0[j]
-    lanes = lax.broadcasted_iota(jnp.int32, (8, 128), 1)
-    used = lanes < 4 * own
+    used = lax.broadcasted_iota(jnp.int32, (1, 128), 1) < 4 * own * n_row
     norm = jnp.where(used, norm, 1.0)
 
     def sent(ref, sem):
         remote(ref, ref, sem, b_recv.at[0, 0], sib).wait_send()
 
-    whole = S.at[0]
+    whole = B.at[0]
 
     @pl.when((d != 6) & (d != 7))
     def _():
@@ -354,7 +328,7 @@
         sent(whole, z_send)
 
     def sib_sent(i, carry):
-        sent(whole, s_send.at[i])
+        send_image(i).wait_send()
         return carry
 
     lax.fori_loop(0, n_slots, sib_sent, 0)
@@ -364,35 +338,44 @@
     for j in range(1, n_col):
         form += R1[j]
     power = jnp.where(used, form / norm, 0.0)
+    stride = own * n_row
     total = power
     for f in range(1, 4):
-        total += pltpu.roll(power, 128 - own * f, 1)
-    both = jnp.where(used, power, pltpu.roll(total, 64, 1))
-    for j in range(n_row):
-        A2[j] = both[j:j + 1]
+        total += pltpu.roll(power, 128 - stride * f, 1)
+    A2[...] = jnp.where(used, power, pltpu.roll(total, 4 * stride, 1))
     me = q * n_row + r
-    R2[me] = A2[r]
+    R2[me] = A2[...]
+    pl.semaphore_wait(gossip.at[ROUNDS - 1], len(near))
 
     def go(j, carry):
         to, at = (r + j) % n_row, (q + j // n_row) % n_freq
-        remote(A2.at[to], R2.at[me], a2_send, a2_recv, (to, c, at)).start()
+        remote(A2, R2.at[me], a2_send, a2_recv, (to, c, at)).start()
         return carry
 
     lax.fori_loop(1, n_row * n_freq, go, 0)
     others = R2.at[pl.ds(1, n_row * n_freq - 1)]
     remote(others, others, a2_send, a2_recv, sib).wait()
-    whole_power = R2[q * n_row]
+    power = R2[q * n_row]
     for j in range(1, n_row):
-        whole_power += R2[q * n_row + j]
+        power += R2[q * n_row + j]
     surface = R2[0]
     for j in range(1, n_row * n_freq):
         surface += R2[j]
-    line = lax.broadcasted_iota(jnp.int32, (4, 128), 0)
-    out = jnp.broadcast_to(whole_power, (4, 128))
-    for f in range(1, 4):
-        out = jnp.where(line == f, pltpu.roll(whole_power, 128 - own * f, 1), out)
-    pow_ref[...] = out[:, 0:own]
-    surf_ref[...] = pltpu.roll(surface, 64, 1)[:, 0:own] / total_freqs
+    mine = (128 - r) % 128
+    power = pltpu.roll(jnp.broadcast_to(power, (8, 128)), mine, 1)
+    surface = pltpu.roll(jnp.broadcast_to(surface, (8, 128)), mine, 1)
+    line = lax.broadcasted_iota(jnp.int32, (8, 128), 0)
+    lane = lax.broadcasted_iota(jnp.int32, (8, 128), 1)
+    out = power
+    for f in range(4):
+        for m in range(own):
+            at = (own * f + m) * n_row - m
+            out = jnp.where((line == f) & (lane == m), pltpu.roll(power, (128 - at) % 128, 1), out)
+    total = surface
+    for m in range(own):
+        total = jnp.where(lane == m, pltpu.roll(surface, 128 - 4 * stride - m * n_row + m, 1), total)
+    pow_ref[...] = out[0:4, 0:own]
+    surf_ref[...] = total[0:1, 0:own] / total_freqs
 
 
 def solution(mesh):
@@ -417,22 +400,22 @@
                 pltpu.VMEM((freqs, 2 * ch, 2 * slab), BF16),
                 pltpu.VMEM((table, slab), BF16),
                 pltpu.VMEM((freqs, 2 * ch, 2 * slab), F32),
+                pltpu.VMEM((freqs, ch, 2 * slab), F32),
                 pltpu.VMEM((3, ch, 2 * slab), BF16),
-                pltpu.VMEM((freqs, ch, 2 * slab), BF16),
                 pltpu.VMEM((freqs, 8, 2 * slab), F32),
                 pltpu.VMEM((freqs, 8, slab), F32),
-                pltpu.VMEM((n_col, n_row, 128), F32),
-                pltpu.VMEM((n_col, n_row, 128), F32),
-                pltpu.VMEM((n_col, n_row, 128), F32),
-                pltpu.VMEM((n_col, n_row, 128), F32),
-                pltpu.VMEM((n_row, 1, 128), F32),
+                pltpu.VMEM((n_col, 1, 128), F32),
+                pltpu.VMEM((n_col, 1, 128), F32),
+                pltpu.VMEM((n_col, 1, 128), F32),
+                pltpu.VMEM((n_col, 1, 128), F32),
+                pltpu.VMEM((1, 128), F32),
                 pltpu.VMEM((n_row * n_freq, 1, 128), F32),
-                dma((4,)), dma((4, 4)), dma((3, NCH)), dma((4, NCH)), dma, dma, dma, dma((4,)),
+                dma((4,)), dma((4, 4)), dma((3, NCH)), dma((4,)), dma, dma, dma, dma((4,)),
                 dma, dma, dma, dma, dma, dma, pltpu.SemaphoreType.REGULAR((ROUNDS,)),
             ],
             compiler_params=pltpu.CompilerParams(
                 collective_id=0, has_side_effects=True, vmem_limit_bytes=63 * 2**20),
-        )(covariance, replica_table, slab_index.reshape(1, slab))
+        )(covariance, replica_table, slab_index)
         return power, surface.reshape(own)
 
     in_specs = (P("freq", None, "row", "col"), P("freq", None, "col", None), P())

time: 53.8 us -> 49.7 us (0.924)
  Pallas kernels: 49.3 us -> 46.5 us
  local copies, waits for them, and re-layouts: 3.63 us -> 2.39 us
    pallas_call x1, Pallas kernels: 49.3 us -> 46.5 us  [local(): pl.pallas_call(functools.partial(kernel, sizes), out_shape=(jax.ShapeDtyp...]
    reshape x1 -> x0, local copies, waits for them, and re-layouts: 1.25 us -> none  [local(): slab_index.reshape(1, slab)]
where the time goes in v4:
time: 49.7 us; the launch traced here: 49.5 us
  Pallas kernels  46.5 us (94%)
  local copies, waits for them, and re-layouts  2.39 us (5%)
  between operations  0.64 us (1%)
    pallas_call x1, Pallas kernels, local(): pl.pallas_call(functools.partial(kernel, sizes), out_shape=(jax.ShapeDtyp...  46.5 us
    unnamed x2, local copies, waits for them, and re-layouts  2.39 us

profile of v4, /device:TPU:1, one launch (start us, length us, event | category | flops | bytes accessed | tf_op | source)
XLA Modules:
  0.0 49.5 jit_solution(15598214181960174831)
XLA Ops:
  0.6 46.5 %shard_map.50 = (f32[4,3]{1,0:T(4,128)}, f32[1,3]{1,0:T(1,128)}) custom-call(bf16[4,2,512,256]{3,2,1,0:T(8,128)(2,1)} %cov.1, bf16[4,2,256,512]{3,2,1,0:T(8,128)(2,1)} %tbl.1, s32[384]{0:T(512)} %idx.1), custom_call_target="tpu_custom_call" | custom-call | tf_op jit(solution)/shard_map/pallas_call | solution.py:392
  47.1 1.2 %copy.7 = f32[4,3]{1,0:T(4,128)} copy(f32[4,3]{1,0:T(4,128)} %get-tuple-element.8) | data formatting | bytes 96
  48.4 1.1 %copy.8 = f32[3]{0:T(128)} copy(f32[3]{0:T(128)} %bitcast.1) | data formatting | bytes 24

commit v5 on v4

--- a/solution.py
+++ b/solution.py
@@ -15,6 +15,10 @@
 MIN_LAG = 8
 GREET = 10
 ROUNDS = 3
+
+
+def mod(a, n):
+    return lax.rem(a, n)
 
 
 def kernel(sizes, cov, tbl, idx, pow_ref, surf_ref,
@@ -26,19 +30,19 @@
     r = lax.axis_index("row")
     c = lax.axis_index("col")
     q = lax.axis_index("freq")
-    y = c // 2
-    k = c % 2
-    zl = r // 4
-    d = (y - r + 8) % 8
-    up = (r, (c + 2) % 16, q)
-    down = (r, (c + 14) % 16, q)
-    mate = ((r + 4) % 8, c, q)
-    up_mate = ((r + 4) % 8, (c + 2) % 16, q)
-    down_mate = ((r + 4) % 8, (c + 14) % 16, q)
+    y = lax.div(c, 2)
+    k = mod(c, 2)
+    zl = lax.div(r, 4)
+    d = mod(y - r + 8, 8)
+    up = (r, mod(c + 2, 16), q)
+    down = (r, mod(c + 14, 16), q)
+    mate = (mod(r + 4, 8), c, q)
+    up_mate = (mod(r + 4, 8), mod(c + 2, 16), q)
+    down_mate = (mod(r + 4, 8), mod(c + 14, 16), q)
     sib = (r, c + 1 - 2 * k, q)
-    across = ((r + 4) % 8, c, (q + jnp.where(zl == 1, 1, n_freq - 1)) % n_freq)
-    column = [(r, (c + j) % n_col, q) for j in range(1, n_col)]
-    rows = [((r + j) % n_row, c, q) for j in range(1, n_row)]
+    across = (mod(r + 4, 8), c, mod(q + jnp.where(zl == 1, 1, n_freq - 1), n_freq))
+    column = [(r, mod(c + j, n_col), q) for j in range(1, n_col)]
+    rows = [(mod(r + j, n_row), c, q) for j in range(1, n_row)]
     near = rows + [across]
 
     barrier = pltpu.get_barrier_semaphore()
@@ -79,17 +83,15 @@
         return carry
 
     lax.fori_loop(0, 4, start_table, 0)
-    lax.fori_loop(0, n_slots, start_cov, 0)
 
     share = slab // n_row
     own = share // n_col
     points = lax.broadcasted_iota(jnp.int32, (table, slab), 0)
     taken = jnp.where(points == idx[...].reshape(1, slab), 1.0, 0.0).astype(BF16)
-    lane = lax.broadcasted_iota(jnp.int32, (slab, slab), 1)
+    lane = lax.broadcasted_iota(jnp.int32, (1, slab), 1)
     source = lane % n_row * share + lane % 128 // n_row * own + lane // 128
     order = jnp.where(lax.broadcasted_iota(jnp.int32, (slab, slab), 0) == source, 1.0, 0.0).astype(BF16)
     OH[...] = jnp.dot(taken, order, preferred_element_type=F32).astype(BF16)
-    ACC[...] = jnp.zeros_like(ACC)
 
     def chunk(j):
         return pl.ds(pl.multiple_of(j * cr, cr), cr)
@@ -121,36 +123,38 @@
     def gather(i, carry):
         table_copy(i).wait()
         both = jnp.dot(T[i].reshape(2 * ch, table), OH[...], preferred_element_type=F32)
-        a, b = both[:ch], both[ch:]
-        na, nb = a.astype(BF16), b.astype(BF16)
+        na, nb = both[:ch].astype(BF16), both[ch:].astype(BF16)
         X[i, 0:ch, 0:slab] = na
         X[i, 0:ch, slab:2 * slab] = nb
         X[i, ch:2 * ch, 0:slab] = -nb
         X[i, ch:2 * ch, slab:2 * slab] = na
 
-        WT[i] = jnp.sum((a * a + b * b).reshape(ch // 8, 8, slab), axis=0)
-
-        @pl.when(i == 0)
+        @pl.when(i == 1)
         def _():
             pl.semaphore_wait(barrier, len(greeted))
 
-        @pl.when(ends & (i == 0))
+        @pl.when(ends & (i == 1))
         def _():
             def go(j, carry):
-                send_up(own_rows(i, j), j).start()
+                send_up(own_rows(0, j), j).start()
+                send_down(own_rows(1, j), j).start()
                 return carry
             lax.fori_loop(0, NCH, go, 0)
 
-        @pl.when(ends & (i == 1))
-        def _():
-            def go(j, carry):
-                send_down(own_rows(i, j), j).start()
-                return carry
-            lax.fori_loop(0, NCH, go, 0)
+        @pl.when(i == 1)
+        def _():
+            lax.fori_loop(0, n_slots, start_cov, 0)
 
         return carry
 
     lax.fori_loop(0, 4, gather, 0)
+    ACC[...] = jnp.zeros_like(ACC)
+
+    def norms(i, carry):
+        w = X[i, 0:ch, :].astype(F32)
+        squares = jnp.sum((w * w).reshape(ch // 8, 8, 2 * slab), axis=0)
+        WT[i] = squares[:, 0:slab] + squares[:, slab:2 * slab]
+        return carry
 
     def image(i, carry):
         for copy in cov_copies(i):
@@ -188,11 +192,9 @@
             to[j] = out[j:j + 1]
 
     def to_column(src, dst, send, recv):
-        def go(j, carry):
-            to = (c + j) % n_col
+        for j in sorted(range(1, n_col), key=lambda j: -min(j // 2, 8 - j // 2)):
+            to = 2 * mod(y + j // 2, 8) + mod(k + j, 2)
             remote(src.at[to], dst.at[j], send, recv, (r, to, q)).start()
-            return carry
-        lax.fori_loop(1, n_col, go, 0)
 
     def column_wait(dst, send, recv):
         others = dst.at[pl.ds(1, n_col - 1)]
@@ -203,6 +205,7 @@
             pl.semaphore_signal(gossip.at[n], inc=1, device_id=to, device_id_type=MESH)
 
     lax.fori_loop(0, n_slots, image, 0)
+    lax.fori_loop(0, 4, norms, 0)
     lines(A0, lambda i: WT[i])
     to_column(A0, R0, a0_send, a0_recv)
     greet(0)
@@ -347,12 +350,11 @@
     R2[me] = A2[...]
     pl.semaphore_wait(gossip.at[ROUNDS - 1], len(near))
 
-    def go(j, carry):
-        to, at = (r + j) % n_row, (q + j // n_row) % n_freq
-        remote(A2, R2.at[me], a2_send, a2_recv, (to, c, at)).start()
-        return carry
-
-    lax.fori_loop(1, n_row * n_freq, go, 0)
+    offsets = [(a, b) for a in range(4) for b in range(8) if a or b]
+    for a, b in sorted(offsets, key=lambda p: -min(p[0], 4 - p[0]) - min(p[1], 8 - p[1])):
+        at_z = mod(2 * q + zl + b, 8)
+        to = (mod(at_z, 2) * 4 + mod(r + a, 4), c, lax.div(at_z, 2))
+        remote(A2, R2.at[me], a2_send, a2_recv, to).start()
     others = R2.at[pl.ds(1, n_row * n_freq - 1)]
     remote(others, others, a2_send, a2_recv, sib).wait()
     power = R2[q * n_row]
@@ -361,7 +363,7 @@
     surface = R2[0]
     for j in range(1, n_row * n_freq):
         surface += R2[j]
-    mine = (128 - r) % 128
+    mine = mod(128 - r, 128)
     power = pltpu.roll(jnp.broadcast_to(power, (8, 128)), mine, 1)
     surface = pltpu.roll(jnp.broadcast_to(surface, (8, 128)), mine, 1)
     line = lax.broadcasted_iota(jnp.int32, (8, 128), 0)
@@ -414,7 +416,7 @@
                 dma, dma, dma, dma, dma, dma, pltpu.SemaphoreType.REGULAR((ROUNDS,)),
             ],
             compiler_params=pltpu.CompilerParams(
-                collective_id=0, has_side_effects=True, vmem_limit_bytes=63 * 2**20),
+                collective_id=0, has_side_effects=True, vmem_limit_bytes=210 * 2**18),
         )(covariance, replica_table, slab_index)
         return power, surface.reshape(own)
 

time: 49.7 us -> 47.3 us (0.952)
  Pallas kernels: 46.5 us -> 44.7 us
  local copies, waits for them, and re-layouts: 2.39 us -> 1.77 us
    pallas_call x1, Pallas kernels: 46.5 us -> 44.7 us  [local(): pl.pallas_call(functools.partial(kernel, sizes), out_shape=(jax.ShapeDtyp...]
    unnamed x2 -> x4, local copies, waits for them, and re-layouts: 2.39 us -> 1.77 us
where the time goes in v5:
time: 47.3 us; the launch traced here: 47.1 us
  Pallas kernels  44.7 us (95%)
  local copies, waits for them, and re-layouts  1.77 us (4%)
  between operations  0.65 us (1%)
    pallas_call x1, Pallas kernels, local(): pl.pallas_call(functools.partial(kernel, sizes), out_shape=(jax.ShapeDtyp...  44.7 us
    unnamed x4, local copies, waits for them, and re-layouts  1.77 us

profile of v5, /device:TPU:1, one launch (start us, length us, event | category | flops | bytes accessed | tf_op | source)
XLA Modules:
  0.0 47.1 jit_solution(12435049367061525265)
XLA Ops:
  0.6 0.0 copy-start
  0.6 0.7 %copy-done = s32[384]{0:T(512)S(1)} copy-done((s32[384]{0:T(512)S(1)}, s32[384]{0:T(512)}, u32[]{:S(2)}) %copy-start) | copy-done | bytes 1560
  1.3 44.7 %shard_map.50 = (f32[4,3]{1,0:T(4,128)S(1)}, f32[1,3]{1,0:T(1,128)S(1)}) custom-call(bf16[4,2,512,256]{3,2,1,0:T(8,128)(2,1)} %cov.1, bf16[4,2,256,512]{3,2,1,0:T(8,128)(2,1)} %tbl.1, s32[384]{0:T(512)S(1)} %copy-done), custom_call_target="tpu_custom_call" | custom-call | tf_op jit(solution)/shard_map/pallas_call | solution.py:394
  46.0 0.6 %copy.7 = f32[4,3]{1,0:T(4,128)} copy(f32[4,3]{1,0:T(4,128)S(1)} %get-tuple-element.8) | data formatting | bytes 96
  46.6 0.5 %copy.8 = f32[3]{0:T(128)} copy(f32[3]{0:T(128)S(1)} %bitcast.1) | data formatting | bytes 24
Async XLA Ops:
  0.6 0.7 %copy-start = (s32[384]{0:T(512)S(1)}, s32[384]{0:T(512)}, u32[]{:S(2)}) copy-start(s32[384]{0:T(512)} %idx.1) | copy-start | bytes 4612
